TPU v7x, 32 devices: a whole 2x2x4 slice. The times are simulated.
32 devices in a mesh: dp: 4 (over y, x), ctx: 8 (over z, core).
Axes of the slice: x: 2, y: 2, z: 4, core: 2. Of those that a mesh axis runs over, the one named last changes fastest.
Arguments:
- inputs: bfloat16 [4, 1024, 4096], P('dp', 'ctx'), may hold values from -8 to 8
- queries: bfloat16 [4, 1024, 8192], P('dp', 'ctx'), may hold values from -256 to 256
- grad_output: bfloat16 [4, 1024, 8192], P('dp', 'ctx'), may hold values from -6 to 6
- kv_weight: bfloat16 [4096, 1024], P(('dp', 'ctx')), may hold values from -1 to 1
Outputs:
- attn_out: bfloat16 [4, 1024, 8192], P('dp', 'ctx')
- grad_query: bfloat16 [4, 1024, 8192], P('dp', 'ctx')
- grad_inputs: bfloat16 [4, 1024, 4096], P('dp', 'ctx')
- grad_weight: float32 [4096, 1024], P(('dp', 'ctx'))
All inputs are finite; a program needn't handle non-finite values.
Results may differ from a plain program's by a relative error of at most 0.035.
Values may be sent and summed in bfloat16 or wider, within the bound.
No kernel may reach another device: no remote copies, remote signals or barrier semaphores. Data moves between devices by JAX's collectives and lax.ppermute only.
A program may use at most 128 MiB of HBM per device.

v0:
```python
import jax
import jax.numpy as jnp
from jax import lax
from jax.sharding import PartitionSpec as P

DH = 128
ROPE_BASE = 500000.0


def shifted(block, axis, distance):
    devices = range(lax.axis_size(axis))
    route = [(i - distance, i) for i in devices if i - distance in devices]
    return lax.ppermute(block, axis, route)


def shifted_2(value, axis, steps):
    count = lax.axis_size(axis)
    pairs = [(source, (source + steps) % count) for source in range(count)]
    return lax.ppermute(value, axis, pairs)


def rope_tables(positions, head_dim):
    half_dim = head_dim // 2
    frequency = ROPE_BASE ** (-2.0 * jnp.arange(half_dim, dtype=jnp.float32) / head_dim)
    angles = positions.astype(jnp.float32)[:, None] * frequency[None, :]
    return (jnp.cos(angles)[:, None, :], jnp.sin(angles)[:, None, :])


def rotary(values, positions):
    half_dim = values.shape[-1] // 2
    cosine, sine_table = rope_tables(positions, values.shape[-1])
    first_half = values[..., :half_dim]
    second = values[..., half_dim:]
    return jnp.concatenate(
        [first_half * cosine - second * sine_table, second * cosine + first_half * sine_table],
        axis=-1,
    )


def rotary_back(gradient, positions):
    half_dim = gradient.shape[-1] // 2
    cosine, sine_table = rope_tables(positions, gradient.shape[-1])
    first_half = gradient[..., :half_dim]
    second = gradient[..., half_dim:]
    return jnp.concatenate(
        [first_half * cosine + second * sine_table, second * cosine - first_half * sine_table],
        axis=-1,
    )


def on_device(inputs, queries, grad_output, kv_weight):
    token_count = inputs.shape[1]
    model_width = inputs.shape[2]
    kv_width = kv_weight.shape[1]
    kv_half = kv_width // 2
    head_dim = DH
    kv_heads = kv_half // head_dim
    q_heads = queries.shape[2] // head_dim
    group_size = q_heads // kv_heads
    row_count = group_size * token_count
    ctx_size = lax.axis_size("ctx")
    data_size = lax.axis_size("dp")
    ctx_index = lax.axis_index("ctx")
    score_scale = head_dim ** (-0.5)
    shard_rows = model_width // (data_size * ctx_size)
    tokens = inputs[0]
    weight_all = lax.all_gather(kv_weight, ("dp", "ctx"), axis=0, tiled=True)
    projected = jnp.dot(tokens, weight_all, preferred_element_type=jnp.float32)
    positions = ctx_index * token_count + jnp.arange(token_count, dtype=jnp.int32)
    key_rows = rotary(
        projected[:, :kv_half].reshape(token_count, kv_heads, head_dim), positions
    ).astype(jnp.bfloat16)
    value_rows = projected[:, kv_half:].astype(jnp.bfloat16)
    own_block = jnp.concatenate([key_rows.reshape(token_count, kv_half), value_rows], axis=1)

    def head_rows(matrix):
        return (
            matrix.reshape(token_count, kv_heads, group_size, head_dim)
            .transpose(1, 2, 0, 3)
            .reshape(kv_heads, row_count, head_dim)
        )

    def token_rows(rows_by_head):
        return (
            rows_by_head.reshape(kv_heads, group_size, token_count, head_dim)
            .transpose(2, 0, 1, 3)
            .reshape(token_count, q_heads * head_dim)
        )

    query_rows = head_rows(queries[0])
    grad_rows = head_rows(grad_output[0])
    query_pos = jnp.arange(row_count, dtype=jnp.int32) % token_count
    key_pos = jnp.arange(token_count, dtype=jnp.int32)

    def split_block(kv_block):
        key_part = kv_block[:, :kv_half].reshape(token_count, kv_heads, head_dim)
        value_part = kv_block[:, kv_half:].reshape(token_count, kv_heads, head_dim)
        return (key_part, value_part)

    def block_scores(key_part, block_id):
        scores = (
            jnp.einsum("hrd,khd->hrk", query_rows, key_part, preferred_element_type=jnp.float32)
            * score_scale
        )
        allowed = (block_id < ctx_index) | (query_pos[:, None] >= key_pos[None, :])
        return (scores, allowed)

    def forward_update(state_now, kv_block, block_id):
        row_top, row_total, row_accum = state_now
        key_part, value_part = split_block(kv_block)
        scores, allowed = block_scores(key_part, block_id)
        scores = jnp.where(allowed[None], scores, -jnp.inf)
        new_top = jnp.maximum(row_top, jnp.max(scores, axis=-1, keepdims=True))
        weights = jnp.exp(scores - new_top)
        factor = jnp.exp(row_top - new_top)
        row_total = row_total * factor + jnp.sum(weights, axis=-1, keepdims=True)
        row_accum = row_accum * factor + jnp.einsum(
            "hrk,khd->hrd",
            weights.astype(jnp.bfloat16),
            value_part,
            preferred_element_type=jnp.float32,
        )
        return (new_top, row_total, row_accum)

    start_state = (
        jnp.full((kv_heads, row_count, 1), -jnp.inf, jnp.float32),
        jnp.zeros((kv_heads, row_count, 1), jnp.float32),
        jnp.zeros((kv_heads, row_count, head_dim), jnp.float32),
    )
    state_now = forward_update(start_state, own_block, ctx_index)
    kv_store = jnp.zeros((ctx_size, token_count, kv_width), jnp.bfloat16)
    kv_store = lax.dynamic_update_slice_in_dim(kv_store, own_block[None], ctx_index, 0)

    def forward_step(offset, loop_state):
        kv_block, stored_now, state_here = loop_state
        kv_block = shifted(kv_block, "ctx", 1)
        source = ctx_index - offset

        def take_block(operands):
            stored, current = operands
            stored = lax.dynamic_update_slice_in_dim(stored, kv_block[None], source, 0)
            return (stored, forward_update(current, kv_block, source))

        def keep_state(operands):
            return operands

        stored_now, state_here = lax.cond(
            offset <= ctx_index, take_block, keep_state, (stored_now, state_here)
        )
        return (kv_block, stored_now, state_here)

    last_block, kv_store, state_now = lax.fori_loop(
        1, ctx_size, forward_step, (own_block, kv_store, state_now)
    )
    row_top, row_total, row_accum = state_now
    attn_rows = (row_accum / row_total).astype(jnp.bfloat16)
    log_total = row_top + jnp.log(row_total)
    row_delta = jnp.sum(
        grad_rows.astype(jnp.float32) * attn_rows.astype(jnp.float32), axis=-1, keepdims=True
    )
    attn_out = token_rows(attn_rows)[None]

    def backward_terms(kv_block, block_id):
        key_part, value_part = split_block(kv_block)
        scores, allowed = block_scores(key_part, block_id)
        probs_now = jnp.where(allowed[None], jnp.exp(scores - log_total), 0.0)
        dprobs = jnp.einsum(
            "hrd,khd->hrk", grad_rows, value_part, preferred_element_type=jnp.float32
        )
        dscores = (probs_now * (dprobs - row_delta)).astype(jnp.bfloat16)
        grad_keys = (
            jnp.einsum("hrk,hrd->khd", dscores, query_rows, preferred_element_type=jnp.float32)
            * score_scale
        )
        grad_values = jnp.einsum(
            "hrk,hrd->khd",
            probs_now.astype(jnp.bfloat16),
            grad_rows,
            preferred_element_type=jnp.float32,
        )
        query_part = jnp.einsum(
            "hrk,khd->hrd", dscores, key_part, preferred_element_type=jnp.float32
        )
        block_grads = jnp.concatenate(
            [grad_keys.reshape(token_count, kv_half), grad_values.reshape(token_count, kv_half)],
            axis=1,
        )
        return (block_grads, query_part)

    def add_block(operands, block_id):
        grad_block, grad_query_sum = operands
        kv_block = lax.dynamic_slice_in_dim(kv_store, block_id, 1, 0)[0]
        block_grads, query_part = backward_terms(kv_block, block_id)
        return (grad_block + block_grads, grad_query_sum + query_part)

    def skip_block(operand_pair):
        return operand_pair

    zero_grads = jnp.zeros((token_count, kv_width), jnp.float32)
    zero_query = jnp.zeros((kv_heads, row_count, head_dim), jnp.float32)

    def backward_step(offset, operands):
        source = ctx_index - offset

        def include(operand_pair):
            return add_block(operand_pair, source)

        grad_block, grad_query_sum = lax.cond(offset <= ctx_index, include, skip_block, operands)
        grad_block = shifted_2(grad_block.astype(jnp.bfloat16), "ctx", 1).astype(grad_block.dtype)
        return (grad_block, grad_query_sum)

    grad_block, grad_query_sum = lax.fori_loop(0, ctx_size, backward_step, (zero_grads, zero_query))
    grad_query = token_rows(grad_query_sum * score_scale).astype(jnp.bfloat16)[None]
    grad_key_rows = rotary_back(
        grad_block[:, :kv_half].reshape(token_count, kv_heads, head_dim), positions
    ).reshape(token_count, kv_half)
    grad_projected = jnp.concatenate([grad_key_rows, grad_block[:, kv_half:]], axis=1).astype(
        jnp.bfloat16
    )
    grad_inputs = lax.dot_general(
        grad_projected, weight_all, (((1,), (1,)), ((), ())), preferred_element_type=jnp.float32
    ).astype(jnp.bfloat16)[None]
    reordered = (
        tokens.reshape(token_count, data_size, ctx_size, shard_rows)
        .transpose(0, 2, 1, 3)
        .reshape(token_count, model_width)
    )
    partial_sum = lax.psum_scatter(
        lax.dot_general(
            reordered, grad_projected, (((0,), (0,)), ((), ())), preferred_element_type=jnp.float32
        ).astype(jnp.bfloat16),
        "ctx",
        scatter_dimension=0,
        tiled=True,
    )
    grad_weight = lax.psum_scatter(partial_sum, "dp", scatter_dimension=0, tiled=True).astype(
        jnp.float32
    )
    return (attn_out, grad_query, grad_inputs, grad_weight)


def solution(mesh):
    in_specs = (
        P("dp", "ctx", None),
        P("dp", "ctx", None),
        P("dp", "ctx", None),
        P(("dp", "ctx"), None),
    )
    out_specs = (
        P("dp", "ctx", None),
        P("dp", "ctx", None),
        P("dp", "ctx", None),
        P(("dp", "ctx"), None),
    )
    return jax.shard_map(
        on_device, mesh=mesh, in_specs=in_specs, out_specs=out_specs, check_vma=False
    )
```

profile of v0, /device:TPU:0, one launch (start us, length us, event | category | flops | bytes accessed | tf_op | source)
XLA Modules:
  0.0 496.9 jit_solution(8035987753920673615)
XLA Ops:
  8.0 3.5 copy.141
  11.5 4.3 copy.110
  15.8 2.3 reshape.240
  18.1 2.2 copy.139
  20.2 3.8 copy.102
  24.1 2.8 reshape.237
  26.9 2.5 copy.107
  29.4 2.3 copy.115
  31.6 2.3 copy.116
  35.2 55.6 %all-gather.2.cloned.1.call-done = bf16[4096,1024]{1,0:T(8,128)(2,1)} async-done(((bf16[128,1024]{1,0:T(8,128)(2,1)}), bf16[4096,1024]{1,0:T(8,128)(2,1)}) %all-gather.2.cloned.1.call-update) | async-done | bytes 8388624 | tf_op jit(solution)/shard_map/all_gather | solution.py:67
  90.8 5.0 fusion.27
  102.1 1.8 copy.101
  103.9 2.1 fusion.41
  106.7 3.3 convolution_add_fusion.1
  111.7 71.5 %while.38 = (s32[]{:T(128)}, bf16[128,1024]{0,1:T(8,128)(2,1)S(1)}, bf16[8,128,1024]{1,2,0:T(8,128)(2,1)}, f32[4,2048,1]{1,0,2:T(4,128)S(1)}, f32[4,2048,1]{1,0,...) while((s32[]{:T(128)}, bf16[128,1024]{0,1:T(8,128)(2,1)S(1)}, ...), condition=%wide.region_7.8_spmd.clone, body=%wide.region_2.7_spmd.clone.sunk | while | flops 551063552 | bytes 61154760 | solution.py:152
  111.7 2.2 collective-permute-start
  115.0 15.1 %collective-permute-start = (bf16[128,1024]{0,1:T(8,128)(2,1)S(1)}, bf16[128,1024]{0,1:T(8,128)(2,1)S(1)}, u32[]{:S(2)}, u32[]{:S(2)}) collective-permute-start(bf16[128,1024]{0,1:T(8,128)(2,1)S(1)} %get-tuple-element.850), channel_id=1, source_target_pairs={{0,1},{1,2},{2,3},{3,4},{4,5},{5,6},{6,7},{8,9},{9,10},{10,11},{11... | collective-permute-start | bytes 786440 | tf_op jit(solution)/shard_map/while/body/eval_jaxpr/ppermute | solution.py:13
  131.3 6.6 %collective-permute-start = (bf16[128,1024]{0,1:T(8,128)(2,1)S(1)}, bf16[128,1024]{0,1:T(8,128)(2,1)S(1)}, u32[]{:S(2)}, u32[]{:S(2)}) collective-permute-start(bf16[128,1024]{0,1:T(8,128)(2,1)S(1)} %get-tuple-element.850), channel_id=1, source_target_pairs={{0,1},{1,2},{2,3},{3,4},{4,5},{5,6},{6,7},{8,9},{9,10},{10,11},{11... | collective-permute-start | bytes 786440 | tf_op jit(solution)/shard_map/while/body/eval_jaxpr/ppermute | solution.py:13
  139.0 16.2 %collective-permute-start = (bf16[128,1024]{0,1:T(8,128)(2,1)S(1)}, bf16[128,1024]{0,1:T(8,128)(2,1)S(1)}, u32[]{:S(2)}, u32[]{:S(2)}) collective-permute-start(bf16[128,1024]{0,1:T(8,128)(2,1)S(1)} %get-tuple-element.850), channel_id=1, source_target_pairs={{0,1},{1,2},{2,3},{3,4},{4,5},{5,6},{6,7},{8,9},{9,10},{10,11},{11... | collective-permute-start | bytes 786440 | tf_op jit(solution)/shard_map/while/body/eval_jaxpr/ppermute | solution.py:13
  156.4 6.6 %collective-permute-start = (bf16[128,1024]{0,1:T(8,128)(2,1)S(1)}, bf16[128,1024]{0,1:T(8,128)(2,1)S(1)}, u32[]{:S(2)}, u32[]{:S(2)}) collective-permute-start(bf16[128,1024]{0,1:T(8,128)(2,1)S(1)} %get-tuple-element.850), channel_id=1, source_target_pairs={{0,1},{1,2},{2,3},{3,4},{4,5},{5,6},{6,7},{8,9},{9,10},{10,11},{11... | collective-permute-start | bytes 786440 | tf_op jit(solution)/shard_map/while/body/eval_jaxpr/ppermute | solution.py:13
  164.2 10.2 %collective-permute-start = (bf16[128,1024]{0,1:T(8,128)(2,1)S(1)}, bf16[128,1024]{0,1:T(8,128)(2,1)S(1)}, u32[]{:S(2)}, u32[]{:S(2)}) collective-permute-start(bf16[128,1024]{0,1:T(8,128)(2,1)S(1)} %get-tuple-element.850), channel_id=1, source_target_pairs={{0,1},{1,2},{2,3},{3,4},{4,5},{5,6},{6,7},{8,9},{9,10},{10,11},{11... | collective-permute-start | bytes 786440 | tf_op jit(solution)/shard_map/while/body/eval_jaxpr/ppermute | solution.py:13
  175.5 6.6 %collective-permute-start = (bf16[128,1024]{0,1:T(8,128)(2,1)S(1)}, bf16[128,1024]{0,1:T(8,128)(2,1)S(1)}, u32[]{:S(2)}, u32[]{:S(2)}) collective-permute-start(bf16[128,1024]{0,1:T(8,128)(2,1)S(1)} %get-tuple-element.850), channel_id=1, source_target_pairs={{0,1},{1,2},{2,3},{3,4},{4,5},{5,6},{6,7},{8,9},{9,10},{10,11},{11... | collective-permute-start | bytes 786440 | tf_op jit(solution)/shard_map/while/body/eval_jaxpr/ppermute | solution.py:13
  183.2 5.4 %copy.108 = f32[4,2048,128]{1,2,0:T(8,128)} copy(f32[4,2048,128]{2,1,0:T(8,128)} %get-tuple-element.456) | data formatting | bytes 8388608 | tf_op jit(solution)/shard_map/while | solution.py:152
  188.7 5.0 %multiply_reduce_fusion = (f32[4,2048]{1,0:T(4,128)S(1)}, bf16[4,2048,128]{1,2,0:T(8,128)(2,1)}) fusion(bf16[4,2048,128]{1,2,0:T(8,128)(2,1)} %reshape.240, f32[4,2048,128]{1,2,0:T(8,128)} %copy.108, f32[4,2048]{1,0:T(4,128)S(1)} %bitcast.152), kind=kLoop, calls=%fused_computation.44 | loop fusion | flops 6283264 | bytes 8454144 | tf_op jit(solution)/shard_map/reduce_sum | solution.py:158
  193.7 2.2 broadcast.182
  195.9 169.3 %while.39 = (s32[]{:T(128)}, f32[128,1024]{0,1:T(8,128)S(1)}, f32[4,2048,128]{2,1,0:T(8,128)}, s32[]{:T(128)}, bf16[8,128,1024]{1,2,0:T(8,128)(2,1)}, /*index=5*...) while((s32[]{:T(128)}, f32[128,1024]{0,1:T(8,128)S(1)}, ...), condition=%wide.region_12.13_spmd.clone, body=%wide.region_9.12_spmd.clone.sunk | while | flops 1351823360 | bytes 85468640 | solution.py:212
  196.0 10.5 %conditional.7 = ((f32[128,1024]{0,1:T(8,128)S(1)}, f32[4,2048,128]{2,1,0:T(8,128)})) conditional(s32[]{:T(128)} %convert_element_type.142, (f32[128,1024]{0,1:T(8,128)S(1)}, f32[4,2048,128]{2,1,0:T(8,128)}) %tuple.112, (s32[]{:T(128)}, s32[]{:T(128)}, s32[2048]{0:T(1024)S(1)}, s32[128]{0:T(128)S(1)}, bf16[8,128,1024]{1,2,0:T(8,128)(2,1)}, ...), branch_computations={%region_10.10_spmd, %region_11.11_spmd.clone} | conditional | flops 1351428096 | bytes 81781416 | solution.py:208
  202.4 2.2 convolution_add_fusion
  204.6 1.9 copy-done.4
  206.5 14.3 %collective-permute-start.1 = (bf16[128,1024]{0,1:T(8,128)(2,1)S(1)}, bf16[128,1024]{0,1:T(8,128)(2,1)S(1)}, u32[]{:S(2)}, u32[]{:S(2)}) collective-permute-start(bf16[128,1024]{0,1:T(8,128)(2,1)S(1)} %convert_element_type.143), channel_id=1, source_target_pairs={{0,1},{1,2},{2,3},{3,4},{4,5},{5,6},{6,7},{7,0},{8,9},{9,10},{10,1... | collective-permute-start | bytes 786440 | tf_op jit(solution)/shard_map/while/body/eval_jaxpr/ppermute | solution.py:19
  220.9 37.2 %collective-permute-done.1 = bf16[128,1024]{0,1:T(8,128)(2,1)S(1)} collective-permute-done((bf16[128,1024]{0,1:T(8,128)(2,1)S(1)}, bf16[128,1024]{0,1:T(8,128)(2,1)S(1)}, u32[]{:S(2)}, u32[]{:S(2)}) %collective-permute-start.1) | collective-permute-done | bytes 262176 | tf_op jit(solution)/shard_map/while/body/eval_jaxpr/ppermute | solution.py:19
  258.3 13.8 %collective-permute-done.1 = bf16[128,1024]{0,1:T(8,128)(2,1)S(1)} collective-permute-done((bf16[128,1024]{0,1:T(8,128)(2,1)S(1)}, bf16[128,1024]{0,1:T(8,128)(2,1)S(1)}, u32[]{:S(2)}, u32[]{:S(2)}) %collective-permute-start.1) | collective-permute-done | bytes 262176 | tf_op jit(solution)/shard_map/while/body/eval_jaxpr/ppermute | solution.py:19
  272.4 13.8 %collective-permute-done.1 = bf16[128,1024]{0,1:T(8,128)(2,1)S(1)} collective-permute-done((bf16[128,1024]{0,1:T(8,128)(2,1)S(1)}, bf16[128,1024]{0,1:T(8,128)(2,1)S(1)}, u32[]{:S(2)}, u32[]{:S(2)}) %collective-permute-start.1) | collective-permute-done | bytes 262176 | tf_op jit(solution)/shard_map/while/body/eval_jaxpr/ppermute | solution.py:19
  286.5 13.8 %collective-permute-done.1 = bf16[128,1024]{0,1:T(8,128)(2,1)S(1)} collective-permute-done((bf16[128,1024]{0,1:T(8,128)(2,1)S(1)}, bf16[128,1024]{0,1:T(8,128)(2,1)S(1)}, u32[]{:S(2)}, u32[]{:S(2)}) %collective-permute-start.1) | collective-permute-done | bytes 262176 | tf_op jit(solution)/shard_map/while/body/eval_jaxpr/ppermute | solution.py:19
  300.6 14.8 %collective-permute-done.1 = bf16[128,1024]{0,1:T(8,128)(2,1)S(1)} collective-permute-done((bf16[128,1024]{0,1:T(8,128)(2,1)S(1)}, bf16[128,1024]{0,1:T(8,128)(2,1)S(1)}, u32[]{:S(2)}, u32[]{:S(2)}) %collective-permute-start.1) | collective-permute-done | bytes 262176 | tf_op jit(solution)/shard_map/while/body/eval_jaxpr/ppermute | solution.py:19
  315.7 16.3 %collective-permute-done.1 = bf16[128,1024]{0,1:T(8,128)(2,1)S(1)} collective-permute-done((bf16[128,1024]{0,1:T(8,128)(2,1)S(1)}, bf16[128,1024]{0,1:T(8,128)(2,1)S(1)}, u32[]{:S(2)}, u32[]{:S(2)}) %collective-permute-start.1) | collective-permute-done | bytes 262176 | tf_op jit(solution)/shard_map/while/body/eval_jaxpr/ppermute | solution.py:19
  332.3 16.3 %collective-permute-done.1 = bf16[128,1024]{0,1:T(8,128)(2,1)S(1)} collective-permute-done((bf16[128,1024]{0,1:T(8,128)(2,1)S(1)}, bf16[128,1024]{0,1:T(8,128)(2,1)S(1)}, u32[]{:S(2)}, u32[]{:S(2)}) %collective-permute-start.1) | collective-permute-done | bytes 262176 | tf_op jit(solution)/shard_map/while/body/eval_jaxpr/ppermute | solution.py:19
  348.9 16.3 %collective-permute-done.1 = bf16[128,1024]{0,1:T(8,128)(2,1)S(1)} collective-permute-done((bf16[128,1024]{0,1:T(8,128)(2,1)S(1)}, bf16[128,1024]{0,1:T(8,128)(2,1)S(1)}, u32[]{:S(2)}, u32[]{:S(2)}) %collective-permute-start.1) | collective-permute-done | bytes 262176 | tf_op jit(solution)/shard_map/while/body/eval_jaxpr/ppermute | solution.py:19
  366.4 5.6 %convert_bitcast_fusion = bf16[4096,1024]{0,1:T(8,128)(2,1)} fusion(bf16[128,4096]{0,1:T(8,128)(2,1)S(1)} %bitcast.151, bf16[128,512]{0,1:T(8,128)(2,1)S(1)} %slice.61, bf16[128,512]{0,1:T(8,128)(2,1)S(1)} %bitcast.158), kind=kOutput, calls=%fused_computation.39 | convolution fusion | flops 1078460416 | bytes 9699328 | tf_op jit(solution)/shard_map/dot_general | solution.py:229
  372.1 86.9 %reduce-scatter.5.cloned.1.call-done = bf16[512,1024]{0,1:T(8,128)(2,1)} async-done(((bf16[4096,1024]{0,1:T(8,128)(2,1)}), bf16[512,1024]{0,1:T(8,128)(2,1)}) %reduce-scatter.5.cloned.1.call-update) | async-done | bytes 1048592 | tf_op jit(solution)/shard_map/reduce_scatter | solution.py:228
  458.9 2.3 copy.131
  461.3 2.2 copy.140
  463.5 3.8 copy.109
  467.2 4.2 broadcast_in_dim_reshape.3
  471.4 2.8 multiply_convert_fusion
  475.6 2.3 convert_element_type.107
  477.9 7.3 %fusion.22 = bf16[1,128,4096]{2,1,0:T(8,128)(2,1)} fusion(bf16[4096,1024]{1,0:T(8,128)(2,1)} %all-gather.2.cloned.1.call-done, bf16[128,512]{0,1:T(8,128)(2,1)S(1)} %slice.61, bf16[128,512]{0,1:T(8,128)(2,1)S(1)} %bitcast.159), kind=kOutput, calls=%fused_computation.41 | convolution fusion | flops 1074790400 | bytes 9699328 | tf_op jit(solution)/shard_map/dot_general | solution.py:220
  485.1 3.2 reduce-scatter.7.cloned.1.call-done
  (171 shorter events, 30.9 us)
Async XLA Ops:
  7.2 83.6 %all-gather.2.cloned.1.call-start = ((), (), s32[]{:S(2)}) async-start(), calls=%async_computation.2 | async-start | bytes 8650752 | tf_op jit(solution)/shard_map/all_gather | solution.py:67
  7.9 451.1 %reduce-scatter.5.cloned.1.call-start = ((), (), s32[]{:S(2)}) async-start(), calls=%async_computation.3 | async-start | bytes 9437184 | tf_op jit(solution)/shard_map/reduce_scatter | solution.py:228
  34.3 64.1 %copy-start.8 = (f32[128,64]{1,0:T(8,128)}, f32[128,64]{1,0:T(8,128)S(1)}, u32[]{:S(2)}) copy-start(f32[128,64]{1,0:T(8,128)S(1)} %get-tuple-element.707) | copy-start | bytes 98308
  34.3 64.1 %copy-start.10 = (f32[128,64]{1,0:T(8,128)}, f32[128,64]{1,0:T(8,128)S(1)}, u32[]{:S(2)}) copy-start(f32[128,64]{1,0:T(8,128)S(1)} %get-tuple-element.708) | copy-start | bytes 98308
  106.7 3.6 copy-start.7
  106.7 5.0 copy-start.12
  110.4 1.3 copy-start.5
  111.7 3.3 collective-permute-start
  115.0 16.2 %collective-permute-start = (bf16[128,1024]{0,1:T(8,128)(2,1)S(1)}, bf16[128,1024]{0,1:T(8,128)(2,1)S(1)}, u32[]{:S(2)}, u32[]{:S(2)}) collective-permute-start(bf16[128,1024]{0,1:T(8,128)(2,1)S(1)} %get-tuple-element.850), channel_id=1, source_target_pairs={{0,1},{1,2},{2,3},{3,4},{4,5},{5,6},{6,7},{8,9},{9,10},{10,11},{11... | collective-permute-start | bytes 786440 | tf_op jit(solution)/shard_map/while/body/eval_jaxpr/ppermute | solution.py:13
  131.3 7.7 %collective-permute-start = (bf16[128,1024]{0,1:T(8,128)(2,1)S(1)}, bf16[128,1024]{0,1:T(8,128)(2,1)S(1)}, u32[]{:S(2)}, u32[]{:S(2)}) collective-permute-start(bf16[128,1024]{0,1:T(8,128)(2,1)S(1)} %get-tuple-element.850), channel_id=1, source_target_pairs={{0,1},{1,2},{2,3},{3,4},{4,5},{5,6},{6,7},{8,9},{9,10},{10,11},{11... | collective-permute-start | bytes 786440 | tf_op jit(solution)/shard_map/while/body/eval_jaxpr/ppermute | solution.py:13
  139.0 17.3 %collective-permute-start = (bf16[128,1024]{0,1:T(8,128)(2,1)S(1)}, bf16[128,1024]{0,1:T(8,128)(2,1)S(1)}, u32[]{:S(2)}, u32[]{:S(2)}) collective-permute-start(bf16[128,1024]{0,1:T(8,128)(2,1)S(1)} %get-tuple-element.850), channel_id=1, source_target_pairs={{0,1},{1,2},{2,3},{3,4},{4,5},{5,6},{6,7},{8,9},{9,10},{10,11},{11... | collective-permute-start | bytes 786440 | tf_op jit(solution)/shard_map/while/body/eval_jaxpr/ppermute | solution.py:13
  156.4 7.7 %collective-permute-start = (bf16[128,1024]{0,1:T(8,128)(2,1)S(1)}, bf16[128,1024]{0,1:T(8,128)(2,1)S(1)}, u32[]{:S(2)}, u32[]{:S(2)}) collective-permute-start(bf16[128,1024]{0,1:T(8,128)(2,1)S(1)} %get-tuple-element.850), channel_id=1, source_target_pairs={{0,1},{1,2},{2,3},{3,4},{4,5},{5,6},{6,7},{8,9},{9,10},{10,11},{11... | collective-permute-start | bytes 786440 | tf_op jit(solution)/shard_map/while/body/eval_jaxpr/ppermute | solution.py:13
  164.2 11.3 %collective-permute-start = (bf16[128,1024]{0,1:T(8,128)(2,1)S(1)}, bf16[128,1024]{0,1:T(8,128)(2,1)S(1)}, u32[]{:S(2)}, u32[]{:S(2)}) collective-permute-start(bf16[128,1024]{0,1:T(8,128)(2,1)S(1)} %get-tuple-element.850), channel_id=1, source_target_pairs={{0,1},{1,2},{2,3},{3,4},{4,5},{5,6},{6,7},{8,9},{9,10},{10,11},{11... | collective-permute-start | bytes 786440 | tf_op jit(solution)/shard_map/while/body/eval_jaxpr/ppermute | solution.py:13
  175.5 7.7 %collective-permute-start = (bf16[128,1024]{0,1:T(8,128)(2,1)S(1)}, bf16[128,1024]{0,1:T(8,128)(2,1)S(1)}, u32[]{:S(2)}, u32[]{:S(2)}) collective-permute-start(bf16[128,1024]{0,1:T(8,128)(2,1)S(1)} %get-tuple-element.850), channel_id=1, source_target_pairs={{0,1},{1,2},{2,3},{3,4},{4,5},{5,6},{6,7},{8,9},{9,10},{10,11},{11... | collective-permute-start | bytes 786440 | tf_op jit(solution)/shard_map/while/body/eval_jaxpr/ppermute | solution.py:13
  195.9 169.7 %copy-start.9 = (f32[128,64]{1,0:T(8,128)S(1)}, f32[128,64]{1,0:T(8,128)}, u32[]{:S(2)}) copy-start(f32[128,64]{1,0:T(8,128)} %copy-done.8) | copy-start | bytes 98308
  195.9 169.7 %copy-start.11 = (f32[128,64]{1,0:T(8,128)S(1)}, f32[128,64]{1,0:T(8,128)}, u32[]{:S(2)}) copy-start(f32[128,64]{1,0:T(8,128)} %copy-done.10) | copy-start | bytes 98308
  197.0 1.7 copy-start
  200.2 2.2 copy-start.3
  204.6 1.9 copy-start.4
  206.5 51.5 %collective-permute-start.1 = (bf16[128,1024]{0,1:T(8,128)(2,1)S(1)}, bf16[128,1024]{0,1:T(8,128)(2,1)S(1)}, u32[]{:S(2)}, u32[]{:S(2)}) collective-permute-start(bf16[128,1024]{0,1:T(8,128)(2,1)S(1)} %convert_element_type.143), channel_id=1, source_target_pairs={{0,1},{1,2},{2,3},{3,4},{4,5},{5,6},{6,7},{7,0},{8,9},{9,10},{10,1... | collective-permute-start | bytes 786440 | tf_op jit(solution)/shard_map/while/body/eval_jaxpr/ppermute | solution.py:19
  258.3 13.9 %collective-permute-start.1 = (bf16[128,1024]{0,1:T(8,128)(2,1)S(1)}, bf16[128,1024]{0,1:T(8,128)(2,1)S(1)}, u32[]{:S(2)}, u32[]{:S(2)}) collective-permute-start(bf16[128,1024]{0,1:T(8,128)(2,1)S(1)} %convert_element_type.143), channel_id=1, source_target_pairs={{0,1},{1,2},{2,3},{3,4},{4,5},{5,6},{6,7},{7,0},{8,9},{9,10},{10,1... | collective-permute-start | bytes 786440 | tf_op jit(solution)/shard_map/while/body/eval_jaxpr/ppermute | solution.py:19
  272.4 13.9 %collective-permute-start.1 = (bf16[128,1024]{0,1:T(8,128)(2,1)S(1)}, bf16[128,1024]{0,1:T(8,128)(2,1)S(1)}, u32[]{:S(2)}, u32[]{:S(2)}) collective-permute-start(bf16[128,1024]{0,1:T(8,128)(2,1)S(1)} %convert_element_type.143), channel_id=1, source_target_pairs={{0,1},{1,2},{2,3},{3,4},{4,5},{5,6},{6,7},{7,0},{8,9},{9,10},{10,1... | collective-permute-start | bytes 786440 | tf_op jit(solution)/shard_map/while/body/eval_jaxpr/ppermute | solution.py:19
  286.5 13.9 %collective-permute-start.1 = (bf16[128,1024]{0,1:T(8,128)(2,1)S(1)}, bf16[128,1024]{0,1:T(8,128)(2,1)S(1)}, u32[]{:S(2)}, u32[]{:S(2)}) collective-permute-start(bf16[128,1024]{0,1:T(8,128)(2,1)S(1)} %convert_element_type.143), channel_id=1, source_target_pairs={{0,1},{1,2},{2,3},{3,4},{4,5},{5,6},{6,7},{7,0},{8,9},{9,10},{10,1... | collective-permute-start | bytes 786440 | tf_op jit(solution)/shard_map/while/body/eval_jaxpr/ppermute | solution.py:19
  300.5 14.9 %collective-permute-start.1 = (bf16[128,1024]{0,1:T(8,128)(2,1)S(1)}, bf16[128,1024]{0,1:T(8,128)(2,1)S(1)}, u32[]{:S(2)}, u32[]{:S(2)}) collective-permute-start(bf16[128,1024]{0,1:T(8,128)(2,1)S(1)} %convert_element_type.143), channel_id=1, source_target_pairs={{0,1},{1,2},{2,3},{3,4},{4,5},{5,6},{6,7},{7,0},{8,9},{9,10},{10,1... | collective-permute-start | bytes 786440 | tf_op jit(solution)/shard_map/while/body/eval_jaxpr/ppermute | solution.py:19
  315.7 16.4 %collective-permute-start.1 = (bf16[128,1024]{0,1:T(8,128)(2,1)S(1)}, bf16[128,1024]{0,1:T(8,128)(2,1)S(1)}, u32[]{:S(2)}, u32[]{:S(2)}) collective-permute-start(bf16[128,1024]{0,1:T(8,128)(2,1)S(1)} %convert_element_type.143), channel_id=1, source_target_pairs={{0,1},{1,2},{2,3},{3,4},{4,5},{5,6},{6,7},{7,0},{8,9},{9,10},{10,1... | collective-permute-start | bytes 786440 | tf_op jit(solution)/shard_map/while/body/eval_jaxpr/ppermute | solution.py:19
  332.2 16.4 %collective-permute-start.1 = (bf16[128,1024]{0,1:T(8,128)(2,1)S(1)}, bf16[128,1024]{0,1:T(8,128)(2,1)S(1)}, u32[]{:S(2)}, u32[]{:S(2)}) collective-permute-start(bf16[128,1024]{0,1:T(8,128)(2,1)S(1)} %convert_element_type.143), channel_id=1, source_target_pairs={{0,1},{1,2},{2,3},{3,4},{4,5},{5,6},{6,7},{7,0},{8,9},{9,10},{10,1... | collective-permute-start | bytes 786440 | tf_op jit(solution)/shard_map/while/body/eval_jaxpr/ppermute | solution.py:19
  348.8 16.4 %collective-permute-start.1 = (bf16[128,1024]{0,1:T(8,128)(2,1)S(1)}, bf16[128,1024]{0,1:T(8,128)(2,1)S(1)}, u32[]{:S(2)}, u32[]{:S(2)}) collective-permute-start(bf16[128,1024]{0,1:T(8,128)(2,1)S(1)} %convert_element_type.143), channel_id=1, source_target_pairs={{0,1},{1,2},{2,3},{3,4},{4,5},{5,6},{6,7},{7,0},{8,9},{9,10},{10,1... | collective-permute-start | bytes 786440 | tf_op jit(solution)/shard_map/while/body/eval_jaxpr/ppermute | solution.py:19
  365.2 1.2 copy-start.6
  372.0 116.3 %reduce-scatter.7.cloned.1.call-start = ((), (), s32[]{:S(2)}) async-start(), calls=%async_computation.4 | async-start | bytes 1310720
Sparse Core Ops, SparseCore 0:
  11.0 79.7 all-gather.1
  372.2 86.7 reduce-scatter.4
  461.8 26.4 reduce-scatter.6
where the time goes:
time: 498 us; the launch traced here: 497 us
  waiting for transfers between devices  297 us (60%)
  starting transfers between devices  78.1 us (16%)
  local copies, waits for them, and re-layouts  65 us (13%)
  matrix products  29 us (6%)
  between operations  14 us (3%)
  other arithmetic  13.1 us (3%)
    ppermute x8, waiting for transfers between devices, shifted_2(): return lax.ppermute(value, axis, pairs)  142 us
    reduce_scatter x1, waiting for transfers between devices, on_device(): lax.psum_scatter(lax.dot_general(reordered, grad_projected, (((0,), (0,))...  86.9 us
    ppermute x7, starting transfers between devices, shifted(): return lax.ppermute(block, axis, route)  63.3 us
    all_gather x1, waiting for transfers between devices, on_device(): weight_all = lax.all_gather(kv_weight, ('dp', 'ctx'), axis=0, tiled=True)  55.6 us
    unnamed x27, local copies, waits for them, and re-layouts  20.9 us
    ppermute x8, starting transfers between devices, shifted_2(): return lax.ppermute(value, axis, pairs)  14.7 us
  transfers between devices with their start and end apart: 18, of which 18 were waited for; matrix products, arithmetic and copies ran while one was open for 10% of the time, Pallas kernels for 0%

commit v1 on v0

--- a/solution.py
+++ b/solution.py
@@ -64,7 +64,15 @@
     score_scale = head_dim ** (-0.5)
     shard_rows = model_width // (data_size * ctx_size)
     tokens = inputs[0]
-    weight_all = lax.all_gather(kv_weight, ("dp", "ctx"), axis=0, tiled=True)
+    ways, here = (lax.axis_size(("dp", "ctx")), lax.axis_index(("dp", "ctx")))
+    grown, reach = (kv_weight, 1)
+    while reach < ways:
+        theirs = lax.ppermute(grown, ("dp", "ctx"), [(d, d ^ reach) for d in range(ways)])
+        mine_first = jnp.concatenate([grown, theirs], axis=0)
+        theirs_first = jnp.concatenate([theirs, grown], axis=0)
+        grown = jnp.where(here & reach == 0, mine_first, theirs_first)
+        reach = 2 * reach
+    weight_all = grown
     projected = jnp.dot(tokens, weight_all, preferred_element_type=jnp.float32)
     positions = ctx_index * token_count + jnp.arange(token_count, dtype=jnp.int32)
     key_rows = rotary(

time: 498 us -> 629 us (1.26)
  waiting for transfers between devices: 297 us -> 412 us
  other arithmetic: 13.1 us -> 22.1 us
  starting transfers between devices: 78.1 us -> 85.1 us
    ppermute x0 -> x5, waiting for transfers between devices: none -> 167 us  [on_device(): lax.ppermute(grown, ('dp', 'ctx'), [(d, d ^ reach) for d in range(ways)])]
    all_gather x1 -> x0, waiting for transfers between devices: 55.6 us -> none  [on_device(): weight_all = lax.all_gather(kv_weight, ('dp', 'ctx'), axis=0, tiled=True)]
    select_n x0 -> x4, other arithmetic: none -> 9.2 us  [on_device(): grown = jnp.where(here & reach == 0, mine_first, theirs_first)]
    ppermute x0 -> x5, starting transfers between devices: none -> 9.1 us  [on_device(): lax.ppermute(grown, ('dp', 'ctx'), [(d, d ^ reach) for d in range(ways)])]
    unnamed x27 -> x18, local copies, waits for them, and re-layouts: 20.9 us -> 19 us
  transfers between devices with their start and end apart: 18 -> 22, of which waited for: 18 -> 22; matrix products, arithmetic and copies ran while one was open for 10% -> 8% of each run, Pallas kernels for 0% -> 0%
where the time goes in v1:
time: 629 us; the launch traced here: 628 us
  waiting for transfers between devices  412 us (66%)
  starting transfers between devices  85.1 us (14%)
  local copies, waits for them, and re-layouts  60.9 us (10%)
  matrix products  32.2 us (5%)
  other arithmetic  22.1 us (4%)
  between operations  14.3 us (2%)
    ppermute x5, waiting for transfers between devices, on_device(): lax.ppermute(grown, ('dp', 'ctx'), [(d, d ^ reach) for d in range(ways)])  167 us
    ppermute x8, waiting for transfers between devices, shifted_2(): return lax.ppermute(value, axis, pairs)  148 us
    reduce_scatter x1, waiting for transfers between devices, on_device(): lax.psum_scatter(lax.dot_general(reordered, grad_projected, (((0,), (0,))...  87.8 us
    ppermute x7, starting transfers between devices, shifted(): return lax.ppermute(block, axis, route)  61.2 us
    unnamed x18, local copies, waits for them, and re-layouts  19 us
    ppermute x8, starting transfers between devices, shifted_2(): return lax.ppermute(value, axis, pairs)  14.7 us
  transfers between devices with their start and end apart: 22, of which 22 were waited for; matrix products, arithmetic and copies ran while one was open for 8% of the time, Pallas kernels for 0%

profile of v1, /device:TPU:0, one launch (start us, length us, event | category | flops | bytes accessed | tf_op | source)
XLA Modules:
  0.0 627.6 jit_solution(3290680269114695586)
XLA Ops:
  10.4 3.0 collective-permute-start.3
  13.4 12.2 %collective-permute-done.3 = bf16[256,1024]{1,0:T(8,128)(2,1)S(1)} collective-permute-done((bf16[256,1024]{1,0:T(8,128)(2,1)S(1)}, bf16[256,1024]{1,0:T(8,128)(2,1)S(1)}, u32[]{:S(2)}, u32[]{:S(2)}) %collective-permute-start.3) | collective-permute-done | bytes 524320 | tf_op jit(solution)/shard_map/ppermute | solution.py:70
  26.1 2.8 collective-permute-start.4
  28.9 45.3 %collective-permute-done.4 = bf16[512,1024]{1,0:T(8,128)(2,1)} collective-permute-done((bf16[512,1024]{1,0:T(8,128)(2,1)S(1)}, bf16[512,1024]{1,0:T(8,128)(2,1)}, u32[]{:S(2)}, u32[]{:S(2)}) %collective-permute-start.4) | collective-permute-done | bytes 1048608 | tf_op jit(solution)/shard_map/ppermute | solution.py:70
  74.3 2.5 maximum_select_fusion.2
  78.3 45.4 %collective-permute-done.5 = bf16[1024,1024]{1,0:T(8,128)(2,1)} collective-permute-done((bf16[1024,1024]{1,0:T(8,128)(2,1)S(1)}, bf16[1024,1024]{1,0:T(8,128)(2,1)}, u32[]{:S(2)}, u32[]{:S(2)}) %collective-permute-start.5) | collective-permute-done | bytes 2097184 | tf_op jit(solution)/shard_map/ppermute | solution.py:70
  123.7 4.9 maximum_select_fusion.1
  129.9 3.5 copy.136
  133.4 4.3 copy.106
  137.7 2.3 reshape.240
  142.2 3.8 copy.99
  146.0 2.8 reshape.237
  148.8 2.6 copy.103
  151.4 2.3 copy.111
  153.6 2.3 copy.112
  157.1 62.6 %collective-permute-done.6 = bf16[2048,1024]{1,0:T(8,128)(2,1)} collective-permute-done((bf16[2048,1024]{1,0:T(8,128)(2,1)}, bf16[2048,1024]{1,0:T(8,128)(2,1)}, u32[]{:S(2)}, u32[]{:S(2)}) %collective-permute-start.6) | collective-permute-done | bytes 4194336 | tf_op jit(solution)/shard_map/ppermute | solution.py:70
  219.6 7.6 %fusion.28 = f32[128,1024]{0,1:T(8,128)S(1)} fusion(bf16[2048,1024]{1,0:T(8,128)(2,1)} %collective-permute-done.6, bf16[2048,1024]{1,0:T(8,128)(2,1)} %maximum_select_fusion.1, pred[]{:T(512)S(6)} %eq.17, bf16[1,128,4096]{2,1,0:T(8,128)(2,1)} %param.12), kind=kOutput, calls=%fused_computation.56 | convolution fusion | flops 1111490560 | bytes 9961473 | tf_op jit(solution)/shard_map/dot_general | solution.py:76
  234.3 3.2 convolution_add_fusion.1
  237.6 69.4 %while.38 = (s32[]{:T(128)}, bf16[128,1024]{0,1:T(8,128)(2,1)S(1)}, bf16[8,128,1024]{1,2,0:T(8,128)(2,1)}, f32[4,2048,1]{1,0,2:T(4,128)S(1)}, f32[4,2048,1]{1,0,...) while((s32[]{:T(128)}, bf16[128,1024]{0,1:T(8,128)(2,1)S(1)}, ...), condition=%wide.region_7.8_spmd.clone, body=%wide.region_2.7_spmd.clone.sunk | while | flops 551063552 | bytes 61154760 | solution.py:160
  240.0 16.7 %collective-permute-start = (bf16[128,1024]{0,1:T(8,128)(2,1)S(1)}, bf16[128,1024]{0,1:T(8,128)(2,1)S(1)}, u32[]{:S(2)}, u32[]{:S(2)}) collective-permute-start(bf16[128,1024]{0,1:T(8,128)(2,1)S(1)} %get-tuple-element.848), channel_id=1, source_target_pairs={{0,1},{1,2},{2,3},{3,4},{4,5},{5,6},{6,7},{8,9},{9,10},{10,11},{11... | collective-permute-start | bytes 786440 | tf_op jit(solution)/shard_map/while/body/eval_jaxpr/ppermute | solution.py:13
  257.9 6.6 %collective-permute-start = (bf16[128,1024]{0,1:T(8,128)(2,1)S(1)}, bf16[128,1024]{0,1:T(8,128)(2,1)S(1)}, u32[]{:S(2)}, u32[]{:S(2)}) collective-permute-start(bf16[128,1024]{0,1:T(8,128)(2,1)S(1)} %get-tuple-element.848), channel_id=1, source_target_pairs={{0,1},{1,2},{2,3},{3,4},{4,5},{5,6},{6,7},{8,9},{9,10},{10,11},{11... | collective-permute-start | bytes 786440 | tf_op jit(solution)/shard_map/while/body/eval_jaxpr/ppermute | solution.py:13
  265.6 16.2 %collective-permute-start = (bf16[128,1024]{0,1:T(8,128)(2,1)S(1)}, bf16[128,1024]{0,1:T(8,128)(2,1)S(1)}, u32[]{:S(2)}, u32[]{:S(2)}) collective-permute-start(bf16[128,1024]{0,1:T(8,128)(2,1)S(1)} %get-tuple-element.848), channel_id=1, source_target_pairs={{0,1},{1,2},{2,3},{3,4},{4,5},{5,6},{6,7},{8,9},{9,10},{10,11},{11... | collective-permute-start | bytes 786440 | tf_op jit(solution)/shard_map/while/body/eval_jaxpr/ppermute | solution.py:13
  283.0 6.6 %collective-permute-start = (bf16[128,1024]{0,1:T(8,128)(2,1)S(1)}, bf16[128,1024]{0,1:T(8,128)(2,1)S(1)}, u32[]{:S(2)}, u32[]{:S(2)}) collective-permute-start(bf16[128,1024]{0,1:T(8,128)(2,1)S(1)} %get-tuple-element.848), channel_id=1, source_target_pairs={{0,1},{1,2},{2,3},{3,4},{4,5},{5,6},{6,7},{8,9},{9,10},{10,11},{11... | collective-permute-start | bytes 786440 | tf_op jit(solution)/shard_map/while/body/eval_jaxpr/ppermute | solution.py:13
  290.7 7.4 %collective-permute-start = (bf16[128,1024]{0,1:T(8,128)(2,1)S(1)}, bf16[128,1024]{0,1:T(8,128)(2,1)S(1)}, u32[]{:S(2)}, u32[]{:S(2)}) collective-permute-start(bf16[128,1024]{0,1:T(8,128)(2,1)S(1)} %get-tuple-element.848), channel_id=1, source_target_pairs={{0,1},{1,2},{2,3},{3,4},{4,5},{5,6},{6,7},{8,9},{9,10},{10,11},{11... | collective-permute-start | bytes 786440 | tf_op jit(solution)/shard_map/while/body/eval_jaxpr/ppermute | solution.py:13
  299.3 6.6 %collective-permute-start = (bf16[128,1024]{0,1:T(8,128)(2,1)S(1)}, bf16[128,1024]{0,1:T(8,128)(2,1)S(1)}, u32[]{:S(2)}, u32[]{:S(2)}) collective-permute-start(bf16[128,1024]{0,1:T(8,128)(2,1)S(1)} %get-tuple-element.848), channel_id=1, source_target_pairs={{0,1},{1,2},{2,3},{3,4},{4,5},{5,6},{6,7},{8,9},{9,10},{10,11},{11... | collective-permute-start | bytes 786440 | tf_op jit(solution)/shard_map/while/body/eval_jaxpr/ppermute | solution.py:13
  307.0 5.5 copy.104
  312.5 5.0 multiply_reduce_fusion
  317.6 2.2 broadcast.182
  319.8 174.8 %while.39 = (s32[]{:T(128)}, f32[128,1024]{0,1:T(8,128)S(1)}, f32[4,2048,128]{2,1,0:T(8,128)}, s32[]{:T(128)}, bf16[8,128,1024]{1,2,0:T(8,128)(2,1)}, /*index=5*...) while((s32[]{:T(128)}, f32[128,1024]{0,1:T(8,128)S(1)}, ...), condition=%wide.region_12.13_spmd.clone, body=%wide.region_9.12_spmd.clone.sunk | while | flops 1351823360 | bytes 85468640 | solution.py:220
  319.9 10.6 %conditional.7 = ((f32[128,1024]{0,1:T(8,128)S(1)}, f32[4,2048,128]{2,1,0:T(8,128)})) conditional(s32[]{:T(128)} %convert_element_type.142, (f32[128,1024]{0,1:T(8,128)S(1)}, f32[4,2048,128]{2,1,0:T(8,128)}) %tuple.111, (s32[]{:T(128)}, s32[]{:T(128)}, s32[2048]{0:T(1024)S(1)}, s32[128]{0:T(128)S(1)}, bf16[8,128,1024]{1,2,0:T(8,128)(2,1)}, ...), branch_computations={%region_10.10_spmd, %region_11.11_spmd.clone} | conditional | flops 1351428096 | bytes 81781416 | solution.py:216
  330.5 14.3 %collective-permute-start.1 = (bf16[128,1024]{0,1:T(8,128)(2,1)S(1)}, bf16[128,1024]{0,1:T(8,128)(2,1)S(1)}, u32[]{:S(2)}, u32[]{:S(2)}) collective-permute-start(bf16[128,1024]{0,1:T(8,128)(2,1)S(1)} %convert_element_type.143), channel_id=1, source_target_pairs={{0,1},{1,2},{2,3},{3,4},{4,5},{5,6},{6,7},{7,0},{8,9},{9,10},{10,1... | collective-permute-start | bytes 786440 | tf_op jit(solution)/shard_map/while/body/eval_jaxpr/ppermute | solution.py:19
  344.8 42.4 %collective-permute-done.1 = bf16[128,1024]{0,1:T(8,128)(2,1)S(1)} collective-permute-done((bf16[128,1024]{0,1:T(8,128)(2,1)S(1)}, bf16[128,1024]{0,1:T(8,128)(2,1)S(1)}, u32[]{:S(2)}, u32[]{:S(2)}) %collective-permute-start.1) | collective-permute-done | bytes 262176 | tf_op jit(solution)/shard_map/while/body/eval_jaxpr/ppermute | solution.py:19
  387.4 13.8 %collective-permute-done.1 = bf16[128,1024]{0,1:T(8,128)(2,1)S(1)} collective-permute-done((bf16[128,1024]{0,1:T(8,128)(2,1)S(1)}, bf16[128,1024]{0,1:T(8,128)(2,1)S(1)}, u32[]{:S(2)}, u32[]{:S(2)}) %collective-permute-start.1) | collective-permute-done | bytes 262176 | tf_op jit(solution)/shard_map/while/body/eval_jaxpr/ppermute | solution.py:19
  401.5 13.8 %collective-permute-done.1 = bf16[128,1024]{0,1:T(8,128)(2,1)S(1)} collective-permute-done((bf16[128,1024]{0,1:T(8,128)(2,1)S(1)}, bf16[128,1024]{0,1:T(8,128)(2,1)S(1)}, u32[]{:S(2)}, u32[]{:S(2)}) %collective-permute-start.1) | collective-permute-done | bytes 262176 | tf_op jit(solution)/shard_map/while/body/eval_jaxpr/ppermute | solution.py:19
  415.6 13.8 %collective-permute-done.1 = bf16[128,1024]{0,1:T(8,128)(2,1)S(1)} collective-permute-done((bf16[128,1024]{0,1:T(8,128)(2,1)S(1)}, bf16[128,1024]{0,1:T(8,128)(2,1)S(1)}, u32[]{:S(2)}, u32[]{:S(2)}) %collective-permute-start.1) | collective-permute-done | bytes 262176 | tf_op jit(solution)/shard_map/while/body/eval_jaxpr/ppermute | solution.py:19
  429.7 14.8 %collective-permute-done.1 = bf16[128,1024]{0,1:T(8,128)(2,1)S(1)} collective-permute-done((bf16[128,1024]{0,1:T(8,128)(2,1)S(1)}, bf16[128,1024]{0,1:T(8,128)(2,1)S(1)}, u32[]{:S(2)}, u32[]{:S(2)}) %collective-permute-start.1) | collective-permute-done | bytes 262176 | tf_op jit(solution)/shard_map/while/body/eval_jaxpr/ppermute | solution.py:19
  444.9 16.3 %collective-permute-done.1 = bf16[128,1024]{0,1:T(8,128)(2,1)S(1)} collective-permute-done((bf16[128,1024]{0,1:T(8,128)(2,1)S(1)}, bf16[128,1024]{0,1:T(8,128)(2,1)S(1)}, u32[]{:S(2)}, u32[]{:S(2)}) %collective-permute-start.1) | collective-permute-done | bytes 262176 | tf_op jit(solution)/shard_map/while/body/eval_jaxpr/ppermute | solution.py:19
  461.4 16.3 %collective-permute-done.1 = bf16[128,1024]{0,1:T(8,128)(2,1)S(1)} collective-permute-done((bf16[128,1024]{0,1:T(8,128)(2,1)S(1)}, bf16[128,1024]{0,1:T(8,128)(2,1)S(1)}, u32[]{:S(2)}, u32[]{:S(2)}) %collective-permute-start.1) | collective-permute-done | bytes 262176 | tf_op jit(solution)/shard_map/while/body/eval_jaxpr/ppermute | solution.py:19
  478.0 16.3 %collective-permute-done.1 = bf16[128,1024]{0,1:T(8,128)(2,1)S(1)} collective-permute-done((bf16[128,1024]{0,1:T(8,128)(2,1)S(1)}, bf16[128,1024]{0,1:T(8,128)(2,1)S(1)}, u32[]{:S(2)}, u32[]{:S(2)}) %collective-permute-start.1) | collective-permute-done | bytes 262176 | tf_op jit(solution)/shard_map/while/body/eval_jaxpr/ppermute | solution.py:19
  495.8 5.6 convert_bitcast_fusion
  501.5 87.8 %reduce-scatter.5.cloned.1.call-done = bf16[512,1024]{0,1:T(8,128)(2,1)} async-done(((bf16[4096,1024]{0,1:T(8,128)(2,1)}), bf16[512,1024]{0,1:T(8,128)(2,1)}) %reduce-scatter.5.cloned.1.call-update) | async-done | bytes 1048592 | tf_op jit(solution)/shard_map/reduce_scatter | solution.py:236
  589.3 2.3 copy.128
  591.6 2.2 copy.135
  593.8 3.8 copy.105
  597.6 4.2 broadcast_in_dim_reshape.3
  601.7 2.8 multiply_convert_fusion
  605.9 2.3 convert_element_type.107
  608.2 9.0 %fusion.22 = bf16[1,128,4096]{2,1,0:T(8,128)(2,1)} fusion(bf16[2048,1024]{1,0:T(8,128)(2,1)} %collective-permute-done.6, bf16[2048,1024]{1,0:T(8,128)(2,1)} %maximum_select_fusion.1, pred[]{:T(512)S(6)} %eq.17, bf16[128,512]{0,1:T(8,128)(2,1)S(1)} %slice.61, bf16[128,512]{0,1:T(8,128)(2,1)S(1)} %bitcast.157), kind=kOutput, calls=%fused_computation.42 | convolution fusion | flops 1112539136 | bytes 9699329 | tf_op jit(solution)/shard_map/dot_general | solution.py:228
  (172 shorter events, 44.0 us)
Async XLA Ops:
  7.2 582.2 %reduce-scatter.5.cloned.1.call-start = ((), (), s32[]{:S(2)}) async-start(), calls=%async_computation.2 | async-start | bytes 9437184 | tf_op jit(solution)/shard_map/reduce_scatter | solution.py:236
  7.2 1.9 collective-permute-start.2
  10.4 15.2 %collective-permute-start.3 = (bf16[256,1024]{1,0:T(8,128)(2,1)S(1)}, bf16[256,1024]{1,0:T(8,128)(2,1)S(1)}, u32[]{:S(2)}, u32[]{:S(2)}) collective-permute-start(bf16[256,1024]{1,0:T(8,128)(2,1)S(1)} %maximum_select_fusion.8), channel_id=1, source_target_pairs={{0,2},{1,3},{2,0},{3,1},{4,6},{5,7},{6,4},{7,5},{8,10},{9,11},{10,... | collective-permute-start | bytes 1572872 | tf_op jit(solution)/shard_map/ppermute | solution.py:70
  26.1 48.2 %collective-permute-start.4 = (bf16[512,1024]{1,0:T(8,128)(2,1)S(1)}, bf16[512,1024]{1,0:T(8,128)(2,1)}, u32[]{:S(2)}, u32[]{:S(2)}) collective-permute-start(bf16[512,1024]{1,0:T(8,128)(2,1)S(1)} %maximum_select_fusion.7), channel_id=1, source_target_pairs={{0,4},{1,5},{2,6},{3,7},{4,0},{5,1},{6,2},{7,3},{8,12},{9,13},{10,... | collective-permute-start | bytes 3145736 | tf_op jit(solution)/shard_map/ppermute | solution.py:70
  76.8 46.8 %collective-permute-start.5 = (bf16[1024,1024]{1,0:T(8,128)(2,1)S(1)}, bf16[1024,1024]{1,0:T(8,128)(2,1)}, u32[]{:S(2)}, u32[]{:S(2)}) collective-permute-start(bf16[1024,1024]{1,0:T(8,128)(2,1)S(1)} %maximum_select_fusion.2), channel_id=1, source_target_pairs={{0,8},{1,9},{2,10},{3,11},{4,12},{5,13},{6,14},{7,15},{8,0},{9,1},... | collective-permute-start | bytes 6291464 | tf_op jit(solution)/shard_map/ppermute | solution.py:70
  128.6 91.1 %collective-permute-start.6 = (bf16[2048,1024]{1,0:T(8,128)(2,1)}, bf16[2048,1024]{1,0:T(8,128)(2,1)}, u32[]{:S(2)}, u32[]{:S(2)}) collective-permute-start(bf16[2048,1024]{1,0:T(8,128)(2,1)} %maximum_select_fusion.1), channel_id=1, source_target_pairs={{0,16},{1,17},{2,18},{3,19},{4,20},{5,21},{6,22},{7,23},{8,24},{9,... | collective-permute-start | bytes 12582920 | tf_op jit(solution)/shard_map/ppermute | solution.py:70
  237.6 2.4 collective-permute-start
  240.0 17.8 %collective-permute-start = (bf16[128,1024]{0,1:T(8,128)(2,1)S(1)}, bf16[128,1024]{0,1:T(8,128)(2,1)S(1)}, u32[]{:S(2)}, u32[]{:S(2)}) collective-permute-start(bf16[128,1024]{0,1:T(8,128)(2,1)S(1)} %get-tuple-element.848), channel_id=1, source_target_pairs={{0,1},{1,2},{2,3},{3,4},{4,5},{5,6},{6,7},{8,9},{9,10},{10,11},{11... | collective-permute-start | bytes 786440 | tf_op jit(solution)/shard_map/while/body/eval_jaxpr/ppermute | solution.py:13
  257.9 7.7 %collective-permute-start = (bf16[128,1024]{0,1:T(8,128)(2,1)S(1)}, bf16[128,1024]{0,1:T(8,128)(2,1)S(1)}, u32[]{:S(2)}, u32[]{:S(2)}) collective-permute-start(bf16[128,1024]{0,1:T(8,128)(2,1)S(1)} %get-tuple-element.848), channel_id=1, source_target_pairs={{0,1},{1,2},{2,3},{3,4},{4,5},{5,6},{6,7},{8,9},{9,10},{10,11},{11... | collective-permute-start | bytes 786440 | tf_op jit(solution)/shard_map/while/body/eval_jaxpr/ppermute | solution.py:13
  265.6 17.3 %collective-permute-start = (bf16[128,1024]{0,1:T(8,128)(2,1)S(1)}, bf16[128,1024]{0,1:T(8,128)(2,1)S(1)}, u32[]{:S(2)}, u32[]{:S(2)}) collective-permute-start(bf16[128,1024]{0,1:T(8,128)(2,1)S(1)} %get-tuple-element.848), channel_id=1, source_target_pairs={{0,1},{1,2},{2,3},{3,4},{4,5},{5,6},{6,7},{8,9},{9,10},{10,11},{11... | collective-permute-start | bytes 786440 | tf_op jit(solution)/shard_map/while/body/eval_jaxpr/ppermute | solution.py:13
  283.0 7.7 %collective-permute-start = (bf16[128,1024]{0,1:T(8,128)(2,1)S(1)}, bf16[128,1024]{0,1:T(8,128)(2,1)S(1)}, u32[]{:S(2)}, u32[]{:S(2)}) collective-permute-start(bf16[128,1024]{0,1:T(8,128)(2,1)S(1)} %get-tuple-element.848), channel_id=1, source_target_pairs={{0,1},{1,2},{2,3},{3,4},{4,5},{5,6},{6,7},{8,9},{9,10},{10,11},{11... | collective-permute-start | bytes 786440 | tf_op jit(solution)/shard_map/while/body/eval_jaxpr/ppermute | solution.py:13
  290.7 8.5 %collective-permute-start = (bf16[128,1024]{0,1:T(8,128)(2,1)S(1)}, bf16[128,1024]{0,1:T(8,128)(2,1)S(1)}, u32[]{:S(2)}, u32[]{:S(2)}) collective-permute-start(bf16[128,1024]{0,1:T(8,128)(2,1)S(1)} %get-tuple-element.848), channel_id=1, source_target_pairs={{0,1},{1,2},{2,3},{3,4},{4,5},{5,6},{6,7},{8,9},{9,10},{10,11},{11... | collective-permute-start | bytes 786440 | tf_op jit(solution)/shard_map/while/body/eval_jaxpr/ppermute | solution.py:13
  299.3 7.7 %collective-permute-start = (bf16[128,1024]{0,1:T(8,128)(2,1)S(1)}, bf16[128,1024]{0,1:T(8,128)(2,1)S(1)}, u32[]{:S(2)}, u32[]{:S(2)}) collective-permute-start(bf16[128,1024]{0,1:T(8,128)(2,1)S(1)} %get-tuple-element.848), channel_id=1, source_target_pairs={{0,1},{1,2},{2,3},{3,4},{4,5},{5,6},{6,7},{8,9},{9,10},{10,11},{11... | collective-permute-start | bytes 786440 | tf_op jit(solution)/shard_map/while/body/eval_jaxpr/ppermute | solution.py:13
  319.8 175.2 %copy-start.6 = (f32[128,64]{1,0:T(8,128)S(1)}, f32[128,64]{1,0:T(8,128)}, u32[]{:S(2)}) copy-start(f32[128,64]{1,0:T(8,128)} %get-tuple-element.705) | copy-start | bytes 98308
  319.8 175.2 %copy-start.7 = (f32[128,64]{1,0:T(8,128)S(1)}, f32[128,64]{1,0:T(8,128)}, u32[]{:S(2)}) copy-start(f32[128,64]{1,0:T(8,128)} %get-tuple-element.706) | copy-start | bytes 98308
  320.9 1.7 copy-start
  324.1 2.2 copy-start.3
  328.5 1.9 copy-start.4
  330.5 56.7 %collective-permute-start.1 = (bf16[128,1024]{0,1:T(8,128)(2,1)S(1)}, bf16[128,1024]{0,1:T(8,128)(2,1)S(1)}, u32[]{:S(2)}, u32[]{:S(2)}) collective-permute-start(bf16[128,1024]{0,1:T(8,128)(2,1)S(1)} %convert_element_type.143), channel_id=1, source_target_pairs={{0,1},{1,2},{2,3},{3,4},{4,5},{5,6},{6,7},{7,0},{8,9},{9,10},{10,1... | collective-permute-start | bytes 786440 | tf_op jit(solution)/shard_map/while/body/eval_jaxpr/ppermute | solution.py:19
  387.3 13.9 %collective-permute-start.1 = (bf16[128,1024]{0,1:T(8,128)(2,1)S(1)}, bf16[128,1024]{0,1:T(8,128)(2,1)S(1)}, u32[]{:S(2)}, u32[]{:S(2)}) collective-permute-start(bf16[128,1024]{0,1:T(8,128)(2,1)S(1)} %convert_element_type.143), channel_id=1, source_target_pairs={{0,1},{1,2},{2,3},{3,4},{4,5},{5,6},{6,7},{7,0},{8,9},{9,10},{10,1... | collective-permute-start | bytes 786440 | tf_op jit(solution)/shard_map/while/body/eval_jaxpr/ppermute | solution.py:19
  401.5 13.9 %collective-permute-start.1 = (bf16[128,1024]{0,1:T(8,128)(2,1)S(1)}, bf16[128,1024]{0,1:T(8,128)(2,1)S(1)}, u32[]{:S(2)}, u32[]{:S(2)}) collective-permute-start(bf16[128,1024]{0,1:T(8,128)(2,1)S(1)} %convert_element_type.143), channel_id=1, source_target_pairs={{0,1},{1,2},{2,3},{3,4},{4,5},{5,6},{6,7},{7,0},{8,9},{9,10},{10,1... | collective-permute-start | bytes 786440 | tf_op jit(solution)/shard_map/while/body/eval_jaxpr/ppermute | solution.py:19
  415.6 13.9 %collective-permute-start.1 = (bf16[128,1024]{0,1:T(8,128)(2,1)S(1)}, bf16[128,1024]{0,1:T(8,128)(2,1)S(1)}, u32[]{:S(2)}, u32[]{:S(2)}) collective-permute-start(bf16[128,1024]{0,1:T(8,128)(2,1)S(1)} %convert_element_type.143), channel_id=1, source_target_pairs={{0,1},{1,2},{2,3},{3,4},{4,5},{5,6},{6,7},{7,0},{8,9},{9,10},{10,1... | collective-permute-start | bytes 786440 | tf_op jit(solution)/shard_map/while/body/eval_jaxpr/ppermute | solution.py:19
  429.7 14.9 %collective-permute-start.1 = (bf16[128,1024]{0,1:T(8,128)(2,1)S(1)}, bf16[128,1024]{0,1:T(8,128)(2,1)S(1)}, u32[]{:S(2)}, u32[]{:S(2)}) collective-permute-start(bf16[128,1024]{0,1:T(8,128)(2,1)S(1)} %convert_element_type.143), channel_id=1, source_target_pairs={{0,1},{1,2},{2,3},{3,4},{4,5},{5,6},{6,7},{7,0},{8,9},{9,10},{10,1... | collective-permute-start | bytes 786440 | tf_op jit(solution)/shard_map/while/body/eval_jaxpr/ppermute | solution.py:19
  444.8 16.4 %collective-permute-start.1 = (bf16[128,1024]{0,1:T(8,128)(2,1)S(1)}, bf16[128,1024]{0,1:T(8,128)(2,1)S(1)}, u32[]{:S(2)}, u32[]{:S(2)}) collective-permute-start(bf16[128,1024]{0,1:T(8,128)(2,1)S(1)} %convert_element_type.143), channel_id=1, source_target_pairs={{0,1},{1,2},{2,3},{3,4},{4,5},{5,6},{6,7},{7,0},{8,9},{9,10},{10,1... | collective-permute-start | bytes 786440 | tf_op jit(solution)/shard_map/while/body/eval_jaxpr/ppermute | solution.py:19
  461.4 16.4 %collective-permute-start.1 = (bf16[128,1024]{0,1:T(8,128)(2,1)S(1)}, bf16[128,1024]{0,1:T(8,128)(2,1)S(1)}, u32[]{:S(2)}, u32[]{:S(2)}) collective-permute-start(bf16[128,1024]{0,1:T(8,128)(2,1)S(1)} %convert_element_type.143), channel_id=1, source_target_pairs={{0,1},{1,2},{2,3},{3,4},{4,5},{5,6},{6,7},{7,0},{8,9},{9,10},{10,1... | collective-permute-start | bytes 786440 | tf_op jit(solution)/shard_map/while/body/eval_jaxpr/ppermute | solution.py:19
  478.0 16.4 %collective-permute-start.1 = (bf16[128,1024]{0,1:T(8,128)(2,1)S(1)}, bf16[128,1024]{0,1:T(8,128)(2,1)S(1)}, u32[]{:S(2)}, u32[]{:S(2)}) collective-permute-start(bf16[128,1024]{0,1:T(8,128)(2,1)S(1)} %convert_element_type.143), channel_id=1, source_target_pairs={{0,1},{1,2},{2,3},{3,4},{4,5},{5,6},{6,7},{7,0},{8,9},{9,10},{10,1... | collective-permute-start | bytes 786440 | tf_op jit(solution)/shard_map/while/body/eval_jaxpr/ppermute | solution.py:19
  494.6 1.2 copy-start.5
  501.4 117.2 %reduce-scatter.7.cloned.1.call-start = ((), (), s32[]{:S(2)}) async-start(), calls=%async_computation.3 | async-start | bytes 1310720
Sparse Core Ops, SparseCore 0:
  501.6 87.7 reduce-scatter.4
  592.2 26.4 reduce-scatter.6
